TPU v7x, 32 devices: a whole 2x2x4 slice. The times are simulated.
32 devices in a mesh: parts: 2 (over y), patch: 4 (over z), sub: 2 (over x), lvl: 2 (over core).
Axes of the slice: x: 2, y: 2, z: 4, core: 2. Of those that a mesh axis runs over, the one named last changes fastest.
Arguments:
- node_states: float32 [8192, 512], P(('parts', 'patch', 'lvl')), parts along dimension 0, may hold values from -6 to 6
- coarse_states: float32 [1024, 512], P(('parts', 'patch', 'lvl')), parts along dimension 0, may hold values from -6 to 6
- children: int32 [512, 7], P(('patch', 'lvl')), may hold values from 0 to 511
- down_sources: int32 [4096, 3], P(('patch', 'lvl')), may hold values from 0 to 63
- bottom_links: int32 [4096, 6], P(('patch', 'lvl')), may hold values from 0 to 767, as said below
- coarse_links: int32 [512, 6], P(('patch', 'lvl')), may hold values from 0 to 511
- upward_sender: float32 [512, 512], P(None, 'sub'), may hold values from -0.25 to 0.25
- upward_receiver: float32 [512, 512], P(None, 'sub'), may hold values from -0.25 to 0.25
- upward_bias: float32 [512], P('sub'), may hold values from -4 to 4
- upward_output: float32 [512, 512], P('sub'), may hold values from -0.25 to 0.25
- upward_gain: float32 [512], replicated, may hold values from 0.1 to 1.9
- coarse_sender: float32 [512, 512], P(None, 'sub'), may hold values from -0.25 to 0.25
- coarse_receiver: float32 [512, 512], P(None, 'sub'), may hold values from -0.25 to 0.25
- coarse_bias: float32 [512], P('sub'), may hold values from -4 to 4
- coarse_output: float32 [512, 512], P('sub'), may hold values from -0.25 to 0.25
- coarse_gain: float32 [512], replicated, may hold values from 0.1 to 1.9
- downward_sender: float32 [512, 512], P(None, 'sub'), may hold values from -0.25 to 0.25
- downward_receiver: float32 [512, 512], P(None, 'sub'), may hold values from -0.25 to 0.25
- downward_bias: float32 [512], P('sub'), may hold values from -4 to 4
- downward_output: float32 [512, 512], P('sub'), may hold values from -0.25 to 0.25
- downward_gain: float32 [512], replicated, may hold values from 0.1 to 1.9
- bottom_sender: float32 [512, 512], P(None, 'sub'), may hold values from -0.25 to 0.25
- bottom_receiver: float32 [512, 512], P(None, 'sub'), may hold values from -0.25 to 0.25
- bottom_bias: float32 [512], P('sub'), may hold values from -4 to 4
- bottom_output: float32 [512, 512], P('sub'), may hold values from -0.25 to 0.25
- bottom_gain: float32 [512], replicated, may hold values from 0.1 to 1.9
Outputs:
- new_nodes: float32 [8192, 512], P(('parts', 'patch', 'lvl')), parts along dimension 0
- new_coarse: float32 [1024, 512], P(('parts', 'patch', 'lvl')), parts along dimension 0
There are 2 independent parts, one for each index of `parts`. A program takes and returns all parts, laid end to end along the dimension named above; an argument that names none is the same for every part. Nothing has to cross between parts.
Inputs may be any that keep to these rules, and one draw needn't show every extreme that they name: bottom_links[n, k] - 128 differs from n's row within its block by at most 128.
All inputs are finite; a program needn't handle non-finite values.
Results may differ from a plain program's by a relative error of at most 0.00011.
Values sent between devices are 32-bit elements; how exact they have to be, the bound alone decides.
A program may use at most 64 MiB of HBM per device.

v0:
```python
import jax
import jax.numpy as jnp
from jax import lax
from jax.sharding import PartitionSpec as P

epsilon = 1e-05
highest = lax.Precision.HIGHEST


def extended(cells, sides, width):
    for axis, dim in sides:
        count = lax.axis_size(axis)
        head = lax.slice_in_dim(cells, 0, width, axis=dim)
        tail = lax.slice_in_dim(cells, cells.shape[dim] - width, cells.shape[dim], axis=dim)
        cells = jnp.concatenate(
            [
                lax.ppermute(tail, axis, [(i, (i + 1) % count) for i in range(count)]),
                cells,
                lax.ppermute(head, axis, [((i + 1) % count, i) for i in range(count)]),
            ],
            axis=dim,
        )
    return cells


def project(states, weights):
    return jnp.dot(states, weights, precision=highest, preferred_element_type=jnp.float32)


def layer_norm(values):
    center = values - jnp.mean(values, axis=-1, keepdims=True)
    spread = jnp.mean(center * center, axis=-1, keepdims=True)
    return center * lax.rsqrt(spread + epsilon)


def hidden_total(picked, receiver_rows):
    return jnp.sum(jax.nn.silu(picked + receiver_rows[:, None, :]), axis=1)


def finish(receivers, hidden, output_weights, gain_vector):
    partial_value = project(hidden, output_weights)
    summed = lax.psum(partial_value, "sub")
    return receivers + gain_vector * layer_norm(summed)


def pick_rows(source_rows, wanted):
    inside = (wanted >= 0) & (wanted < source_rows.shape[0])
    picked = jnp.take(source_rows, jnp.clip(wanted, 0, source_rows.shape[0] - 1), axis=0)
    return jnp.where(inside[:, None], picked, 0.0)


def body(
    node_states,
    coarse_states,
    children,
    down_sources,
    bottom_links,
    coarse_links,
    upward_sender,
    upward_receiver,
    upward_bias,
    upward_output,
    upward_gain,
    coarse_sender,
    coarse_receiver,
    coarse_bias,
    coarse_output,
    coarse_gain,
    downward_sender,
    downward_receiver,
    downward_bias,
    downward_output,
    downward_gain,
    bottom_sender,
    bottom_receiver,
    bottom_bias,
    bottom_output,
    bottom_gain,
):
    sender_rows = project(node_states, upward_sender)
    receiver_rows = project(coarse_states, upward_receiver) + upward_bias
    picked = jnp.take(sender_rows, children, axis=0)
    coarse_up = finish(
        coarse_states, hidden_total(picked, receiver_rows), upward_output, upward_gain
    )
    receiver_rows = project(coarse_up, coarse_receiver) + coarse_bias
    flat_links = coarse_links.reshape(-1)
    own_projection = project(coarse_up, coarse_sender)
    gathered = pick_rows(
        lax.all_gather(own_projection, ("patch", "lvl"), axis=0, tiled=True), flat_links
    )
    picked = gathered.reshape(coarse_links.shape[0], coarse_links.shape[1], receiver_rows.shape[1])
    new_coarse = finish(coarse_up, hidden_total(picked, receiver_rows), coarse_output, coarse_gain)
    sender_rows = project(new_coarse, downward_sender)
    receiver_rows = project(node_states, downward_receiver) + downward_bias
    picked = jnp.take(sender_rows, down_sources, axis=0)
    nodes_down = finish(
        node_states, hidden_total(picked, receiver_rows), downward_output, downward_gain
    )
    rim_rows = node_states.shape[0] // 4
    receiver_rows = project(nodes_down, bottom_receiver) + bottom_bias
    own_projection = project(nodes_down, bottom_sender)
    sender_rows = extended(own_projection, ((("patch", "lvl"), 0),), rim_rows)
    picked = jnp.take(sender_rows, bottom_links, axis=0)
    new_nodes = finish(nodes_down, hidden_total(picked, receiver_rows), bottom_output, bottom_gain)
    return (new_nodes, new_coarse)


def solution(mesh):
    in_specs = (
        P(("parts", "patch", "lvl"), None),
        P(("parts", "patch", "lvl"), None),
        P(("patch", "lvl"), None),
        P(("patch", "lvl"), None),
        P(("patch", "lvl"), None),
        P(("patch", "lvl"), None),
        P(None, "sub"),
        P(None, "sub"),
        P("sub"),
        P("sub", None),
        P(),
        P(None, "sub"),
        P(None, "sub"),
        P("sub"),
        P("sub", None),
        P(),
        P(None, "sub"),
        P(None, "sub"),
        P("sub"),
        P("sub", None),
        P(),
        P(None, "sub"),
        P(None, "sub"),
        P("sub"),
        P("sub", None),
        P(),
    )
    out_specs = (P(("parts", "patch", "lvl"), None), P(("parts", "patch", "lvl"), None))
    return jax.shard_map(body, mesh=mesh, in_specs=in_specs, out_specs=out_specs, check_vma=False)
```

profile of v0, /device:TPU:0, one launch (start us, length us, event | category | flops | bytes accessed | tf_op | source)
XLA Modules:
  0.0 235.3 jit_solution(15321210769861987477)
XLA Ops:
  7.2 0.0 all-reduce.5.cloned.1.call-start
  7.2 0.7 compare_select_fusion.3
  8.0 0.7 compare_and_fusion.4
  8.7 0.1 copy.35
  8.8 0.1 reshape.129
  8.9 2.3 fusion.3
  11.3 1.7 gather_fusion
  13.1 0.1 reshape.128
  13.1 0.1 copy.34
  13.3 0.4 convolution_add_fusion.3
  13.7 0.3 multiply_reduce_fusion.4
  14.0 2.1 fusion.4
  16.2 0.0 all-reduce.7.cloned.1.call-start
  16.3 0.1 copy.38
  16.4 0.1 min.12
  16.6 2.0 convolution_add_fusion.1
  18.6 0.1 copy.36
  18.7 0.1 copy.37
  18.9 21.8 %all-reduce.5.cloned.1.call-done = f32[64,512]{1,0:T(8,128)} async-done(((f32[64,512]{1,0:T(8,128)}), f32[64,512]{1,0:T(8,128)}) %all-reduce.5.cloned.1.call-update) | async-done | bytes 131088 | tf_op jit(solution)/shard_map/psum | solution.py:42
  40.6 1.0 reduce_sum.109
  41.6 1.1 multiply_reduce_fusion.6
  42.8 1.0 multiply_add_fusion.3
  43.8 0.4 fusion.5
  44.2 14.7 %all_gather.3 = f32[512,256]{1,0:T(8,128)S(1)} all-gather(f32[64,256]{1,0:T(8,128)S(1)} %fusion.5), channel_id=1, replica_groups=mesh['parts'=2,'patch'=4,'sub'=2,'lvl'=2] {'patch','lvl'}, dimensions={0}, use_global_device_ids=true | all-gather | bytes 589824 | tf_op jit(solution)/shard_map/all_gather | solution.py:90
  58.9 1.7 gather_fusion.1
  60.5 0.1 gather.20
  60.6 1.5 convolution_add_fusion.2
  62.1 0.5 multiply_reduce_fusion.3
  62.6 2.1 fusion.6
  64.8 0.0 all-reduce.9.cloned.1.call-start
  64.8 0.1 copy.39
  65.0 0.2 reshape.145
  65.2 0.2 copy.33
  65.4 21.2 %all-reduce.7.cloned.1.call-done = f32[64,512]{1,0:T(8,128)} async-done(((f32[64,512]{1,0:T(8,128)}), f32[64,512]{1,0:T(8,128)}) %all-reduce.7.cloned.1.call-update) | async-done | bytes 131088 | tf_op jit(solution)/shard_map/psum | solution.py:42
  86.6 1.0 reduce_sum.112
  87.7 1.1 multiply_reduce_fusion.5
  88.8 1.0 multiply_add_fusion.2
  89.8 0.4 fusion.7
  90.2 4.7 %gather_fusion.2 = f32[1536,256]{1,0:T(8,128)} fusion(f32[64,256]{1,0:T(8,128)S(1)} %fusion.7, s32[2048]{0:T(1024)S(1)} %pad_clamp_fusion), kind=kCustom, calls=%fused_computation.2 | custom fusion | bytes 3151872 | tf_op jit(solution)/shard_map/jit(_take)/gather | solution.py:96
  94.9 3.6 %reshape.144 = f32[512,3,256]{2,1,0:T(4,128)} reshape(f32[1536,256]{1,0:T(8,128)} %gather_fusion.2) | data formatting | bytes 3145728 | tf_op jit(solution)/shard_map/jit(_take)/gather | solution.py:96
  98.5 4.4 %fusion = f32[512,256]{1,0:T(8,128)S(1)} fusion(f32[512,3,256]{2,1,0:T(4,128)} %reshape.144, f32[512,256]{1,0:T(8,128)S(1)} %convolution_add_fusion.1, pred[512,3]{1,0:T(8,128)(4,1)S(1)} %copy.33), kind=kLoop, calls=%fused_computation.6 | loop fusion | flops 2621440 | bytes 2622976 | tf_op jit(solution)/shard_map/reduce_sum | solution.py:37
  103.0 2.0 fusion.8
  105.0 0.2 all-reduce.11.cloned.1.call-start
  105.2 0.1 copy.41
  105.4 0.2 reshape.153
  105.6 0.2 copy.40
  105.8 39.4 %all-reduce.9.cloned.1.call-done = f32[512,512]{1,0:T(8,128)} async-done(((f32[512,512]{1,0:T(8,128)}), f32[512,512]{1,0:T(8,128)}) %all-reduce.9.cloned.1.call-update) | async-done | bytes 1048592 | tf_op jit(solution)/shard_map/psum | solution.py:42
  145.2 1.4 reduce_sum.115
  146.6 1.5 multiply_reduce_fusion.2
  148.1 1.5 multiply_add_fusion.1
  149.6 1.0 fusion.9
  150.7 0.1 collective-permute-start
  150.7 3.5 %collective-permute-start.1 = (f32[128,256]{1,0:T(8,128)S(1)}, f32[128,256]{1,0:T(8,128)S(1)}, u32[]{:S(2)}, u32[]{:S(2)}) collective-permute-start(f32[128,256]{1,0:T(8,128)S(1)} %get-tuple-element.3), channel_id=1, source_target_pairs={{1,0},{4,1},{5,4},{8,5},{9,8},{12,9},{13,12},{0,13},{3,2},{6,3},{7... | collective-permute-start | bytes 393224 | tf_op jit(solution)/shard_map/ppermute | solution.py:19
  154.3 1.0 convolution_add_fusion
  155.3 1.7 collective-permute-done
  157.0 0.1 pad_maximum_fusion
  157.1 12.3 %gather_fusion.3 = f32[3072,256]{1,0:T(8,128)} fusion(f32[768,256]{1,0:T(8,128)S(1)} %pad_maximum_fusion, s32[3072]{0:T(1024)S(1)} %broadcast_clamp_fusion), kind=kCustom, calls=%fused_computation.3 | custom fusion | bytes 6303744 | tf_op jit(solution)/shard_map/jit(_take)/gather | solution.py:104
  169.4 4.5 %reshape.152 = f32[512,6,256]{2,1,0:T(8,128)} reshape(f32[3072,256]{1,0:T(8,128)} %gather_fusion.3) | data formatting | bytes 6291456 | tf_op jit(solution)/shard_map/jit(_take)/gather | solution.py:104
  173.9 7.1 %multiply_reduce_fusion = f32[512,256]{1,0:T(8,128)S(1)} fusion(f32[512,6,256]{2,1,0:T(8,128)} %reshape.152, f32[512,256]{1,0:T(8,128)S(1)} %convolution_add_fusion, pred[512,6]{1,0:T(8,128)(4,1)S(1)} %copy.40), kind=kLoop, calls=%fused_computation.4 | loop fusion | flops 5373952 | bytes 4197376 | tf_op jit(solution)/shard_map/reduce_sum | solution.py:37
  181.1 2.0 fusion.10
  183.1 40.4 %all-reduce.11.cloned.1.call-done = f32[512,512]{1,0:T(8,128)} async-done(((f32[512,512]{1,0:T(8,128)}), f32[512,512]{1,0:T(8,128)}) %all-reduce.11.cloned.1.call-update) | async-done | bytes 1048592 | tf_op jit(solution)/shard_map/psum | solution.py:42
  223.5 1.4 reduce_sum.118
  224.9 1.5 multiply_reduce_fusion.1
  226.4 2.4 %multiply_add_fusion = f32[512,512]{1,0:T(8,128)} fusion(f32[512,512]{1,0:T(8,128)S(1)} %multiply_add_fusion.1, f32[512,512]{1,0:T(8,128)} %all-reduce.11.cloned.1.call-done, f32[512]{0:T(512)S(1)} %add_rsqrt_fusion, f32[512]{0:T(512)S(1)} %broadcast_multiply_fusion, f32[512]{0:T(512)S(1)} %copy-done.16), kind=kLoop, calls=%fused_computation.11 | loop fusion | flops 1048576 | bytes 3151872 | tf_op jit(solution)/shard_map/add | solution.py:43
  (67 shorter events, 0.3 us)
Async XLA Ops:
  7.2 95.8 %copy-start = (f32[256,512]{1,0:T(8,128)S(1)}, f32[256,512]{1,0:T(8,128)}, u32[]{:S(2)}) copy-start(f32[256,512]{1,0:T(8,128)} %param.45) | copy-start | bytes 1572868
  7.2 33.4 %all-reduce.5.cloned.1.call-start = ((), (), s32[]{:S(2)}) async-start(), calls=%async_computation | async-start | bytes 262144 | tf_op jit(solution)/shard_map/psum | solution.py:42
  11.3 2.0 copy-start.2
  11.3 2.0 copy-start.5
  11.3 2.0 copy-start.17
  11.3 4.9 %copy-start.12 = (s32[64,6]{0,1:T(8,128)S(1)}, s32[64,6]{0,1:T(8,128)}, u32[]{:S(2)}) copy-start(s32[64,6]{0,1:T(8,128)} %param.31) | copy-start | bytes 4612
  11.3 5.2 %copy-start.11 = (s32[512,3]{0,1:T(4,128)S(1)}, s32[512,3]{0,1:T(4,128)}, u32[]{:S(2)}) copy-start(s32[512,3]{0,1:T(4,128)} %param.29) | copy-start | bytes 18436
  11.3 5.2 %copy-start.1 = (f32[512,512]{1,0:T(8,128)S(1)}, f32[512,512]{1,0:T(8,128)}, u32[]{:S(2)}) copy-start(f32[512,512]{1,0:T(8,128)} %param.26) | copy-start | bytes 3145732
  11.3 5.2 %copy-start.18 = (f32[256]{0:T(256)S(1)}, f32[256]{0:T(256)}, u32[]{:S(2)}) copy-start(f32[256]{0:T(256)} %param.44) | copy-start | bytes 3076
  13.1 29.7 %copy-start.13 = (f32[512]{0:T(512)S(1)}, f32[512]{0:T(512)}, u32[]{:S(2)}) copy-start(f32[512]{0:T(512)} %param.36) | copy-start | bytes 6148
  13.7 30.1 %copy-start.3 = (f32[512,256]{1,0:T(8,128)S(1)}, f32[512,256]{1,0:T(8,128)}, u32[]{:S(2)}) copy-start(f32[512,256]{1,0:T(8,128)} %param.37) | copy-start | bytes 1572868
  16.2 70.4 %all-reduce.7.cloned.1.call-start = ((), (), s32[]{:S(2)}) async-start(), calls=%async_computation.1 | async-start | bytes 262144 | tf_op jit(solution)/shard_map/psum | solution.py:42
  41.6 19.0 %copy-start.19 = (f32[256]{0:T(256)S(1)}, f32[256]{0:T(256)}, u32[]{:S(2)}) copy-start(f32[256]{0:T(256)} %param.39) | copy-start | bytes 3076
  58.9 29.9 %copy-start.14 = (f32[512]{0:T(512)S(1)}, f32[512]{0:T(512)}, u32[]{:S(2)}) copy-start(f32[512]{0:T(512)} %param.41) | copy-start | bytes 6148
  60.6 29.2 %copy-start.4 = (f32[512,256]{1,0:T(8,128)S(1)}, f32[512,256]{1,0:T(8,128)}, u32[]{:S(2)}) copy-start(f32[512,256]{1,0:T(8,128)} %param.42) | copy-start | bytes 1572868
  64.8 80.5 %all-reduce.9.cloned.1.call-start = ((), (), s32[]{:S(2)}) async-start(), calls=%async_computation.2 | async-start | bytes 2097152 | tf_op jit(solution)/shard_map/psum | solution.py:42
  89.8 5.1 %copy-start.6 = (f32[64,512]{1,0:T(8,128)}, f32[64,512]{1,0:T(8,128)S(1)}, u32[]{:S(2)}) copy-start(f32[64,512]{1,0:T(8,128)S(1)} %multiply_add_fusion.2) | copy-start | bytes 393220
  98.5 6.7 %copy-start.10 = (s32[512,6]{0,1:T(8,128)S(1)}, s32[512,6]{0,1:T(8,128)}, u32[]{:S(2)}) copy-start(s32[512,6]{0,1:T(8,128)} %param.30) | copy-start | bytes 36868
  102.9 45.2 %copy-start.15 = (f32[512]{0:T(512)S(1)}, f32[512]{0:T(512)}, u32[]{:S(2)}) copy-start(f32[512]{0:T(512)} %param.46) | copy-start | bytes 6148
  105.0 44.7 %copy-start.7 = (f32[512,256]{1,0:T(8,128)S(1)}, f32[512,256]{1,0:T(8,128)}, u32[]{:S(2)}) copy-start(f32[512,256]{1,0:T(8,128)} %param.47) | copy-start | bytes 1572868
  105.0 118.5 %all-reduce.11.cloned.1.call-start = ((), (), s32[]{:S(2)}) async-start(), calls=%async_computation.3 | async-start | bytes 2097152 | tf_op jit(solution)/shard_map/psum | solution.py:42
  148.1 6.2 %copy-start.8 = (f32[512,256]{1,0:T(8,128)S(1)}, f32[512,256]{1,0:T(8,128)}, u32[]{:S(2)}) copy-start(f32[512,256]{1,0:T(8,128)} %param.48) | copy-start | bytes 1572868
  148.1 6.2 %copy-start.20 = (f32[256]{0:T(256)S(1)}, f32[256]{0:T(256)}, u32[]{:S(2)}) copy-start(f32[256]{0:T(256)} %param.49) | copy-start | bytes 3076
  150.7 6.3 %collective-permute-start = (f32[128,256]{1,0:T(8,128)S(1)}, f32[128,256]{1,0:T(8,128)S(1)}, u32[]{:S(2)}, u32[]{:S(2)}) collective-permute-start(f32[128,256]{1,0:T(8,128)S(1)} %get-tuple-element.2), channel_id=1, source_target_pairs={{0,1},{1,4},{4,5},{5,8},{8,9},{9,12},{12,13},{13,0},{2,3},{3,6},{6... | collective-permute-start | bytes 393224 | tf_op jit(solution)/shard_map/ppermute | solution.py:17
  150.7 6.3 %collective-permute-start.1 = (f32[128,256]{1,0:T(8,128)S(1)}, f32[128,256]{1,0:T(8,128)S(1)}, u32[]{:S(2)}, u32[]{:S(2)}) collective-permute-start(f32[128,256]{1,0:T(8,128)S(1)} %get-tuple-element.3), channel_id=1, source_target_pairs={{1,0},{4,1},{5,4},{8,5},{9,8},{12,9},{13,12},{0,13},{3,2},{6,3},{7... | collective-permute-start | bytes 393224 | tf_op jit(solution)/shard_map/ppermute | solution.py:19
  173.9 7.1 %copy-start.9 = (f32[256,512]{1,0:T(8,128)S(1)}, f32[256,512]{1,0:T(8,128)}, u32[]{:S(2)}) copy-start(f32[256,512]{1,0:T(8,128)} %param.50) | copy-start | bytes 1572868
  181.1 45.3 %copy-start.16 = (f32[512]{0:T(512)S(1)}, f32[512]{0:T(512)}, u32[]{:S(2)}) copy-start(f32[512]{0:T(512)} %param.51) | copy-start | bytes 6148
Sparse Core Ops, SparseCore 0:
  16.3 24.2 all-reduce.4
  64.9 21.6 all-reduce.6
  105.1 40.0 all-reduce.8
  183.2 40.2 all-reduce.10
where the time goes:
time: 236 us; the launch traced here: 235 us
  waiting for transfers between devices  125 us (53%)
  local copies, waits for them, and re-layouts  30.7 us (13%)
  other arithmetic  29.8 us (13%)
  matrix products  17.2 us (7%)
  blocking collectives  14.7 us (6%)
  between operations  14.4 us (6%)
  starting transfers between devices  3.93 us (2%)
    psum x4, waiting for transfers between devices, finish(): summed = lax.psum(partial_value, 'sub')  123 us
    dot_general x12, matrix products, project(): jnp.dot(states, weights, precision=highest, preferred_element_type=jnp.fl...  17.2 us
    gather x2, local copies, waits for them, and re-layouts, body(): picked = jnp.take(sender_rows, bottom_links, axis=0)  16.9 us
    all_gather x1, blocking collectives, body(): lax.all_gather(own_projection, ('patch', 'lvl'), axis=0, tiled=True)  14.7 us
    reduce_sum x4, other arithmetic, hidden_total(): return jnp.sum(jax.nn.silu(picked + receiver_rows[:, None, :]), axis=1)  12.4 us
    gather x2, local copies, waits for them, and re-layouts, body(): picked = jnp.take(sender_rows, down_sources, axis=0)  8.31 us
    add x4, other arithmetic, finish(): return receivers + gain_vector * layer_norm(summed)  5.93 us
    reduce_sum x4, other arithmetic, layer_norm(): spread = jnp.mean(center * center, axis=-1, keepdims=True)  5.13 us
  transfers between devices with their start and end apart: 6, of which 5 were waited for; matrix products, arithmetic and copies ran while one was open for 2% of the time, Pallas kernels for 0%

commit v1 on v0

v1 whole, which is shorter than its diff:
```python
import functools

import jax
import jax.numpy as jnp
from jax import lax
from jax.experimental import pallas as pl
from jax.experimental.pallas import tpu as pltpu
from jax.sharding import PartitionSpec as P

epsilon = 1e-05
f32 = jnp.float32
bf16 = jnp.bfloat16
MESH = pl.DeviceIdType.MESH


def split(x):
    high = x.astype(bf16)
    return high, (x - high.astype(f32)).astype(bf16)


def mm(a, b):
    return jnp.dot(a, b, preferred_element_type=f32)


def dot3(x, w):
    return mm(x[0], w[0]) + (mm(x[0], w[1]) + mm(x[1], w[0]))


def layer_norm(values):
    center = values - jnp.mean(values, axis=-1, keepdims=True)
    spread = jnp.mean(center * center, axis=-1, keepdims=True)
    return center * lax.rsqrt(spread + epsilon)


def silu(v):
    h = 0.5 * v
    return h + h * jnp.tanh(h)


def joined(pair):
    return jnp.concatenate(pair, axis=1)


def pick(column, table, base):
    count, width = table.shape[0], table.shape[1] // 2
    lanes = lax.broadcasted_iota(jnp.int32, (column.shape[0], count), 1)
    hot = jnp.where(lanes == column - base, 1.0, 0.0).astype(bf16)
    rows = mm(hot, table)
    return rows[:, :width] + rows[:, width:]


def kernel(
    n_patch,
    n_sub,
    n_lvl,
    rim,
    tile,
    nodes_hbm,
    coarse_hbm,
    us_hbm, ur_hbm, uo_hbm,
    cs_hbm, cr_hbm, co_hbm,
    ds_hbm, dr_hbm, do_hbm,
    bs_hbm, br_hbm, bo_hbm,
    children, down_sources, bottom_links, coarse_links,
    ub, ug, cb, cg, db, dg, bb, bg,
    out_nodes,
    out_coarse,
    ns, cs, w_in, w_mid, wo_full, wo_pair, bw_pair,
    ns_pair, rd, rb, nd, ext, halo_out, halo_in,
    table, parts, hidden,
    load_sem, wo_send, wo_recv, fw_send, fw_recv,
    part_send, part_recv, tab_send, tab_recv, rel_send, rel_recv,
    hid_send, hid_recv, halo_send, halo_recv,
):
    patch = lax.axis_index("patch")
    sub = lax.axis_index("sub")
    lvl = lax.axis_index("lvl")
    rows = ns.shape[0]
    width = table.shape[2]
    tiles = rows // tile
    block = patch * n_lvl + lvl
    blocks = n_patch * n_lvl

    def at_sub(o):
        return {"sub": lax.rem(sub + o, n_sub)}

    def at_lvl(o):
        return {"lvl": lax.rem(lvl + o, n_lvl)}

    def at_patch(o):
        return {"patch": lax.rem(patch + o, n_patch)}

    def at_block(o):
        other = lax.rem(block + o + blocks, blocks)
        return {"patch": other // n_lvl, "lvl": lax.rem(other, n_lvl)}

    def from_sub(o):
        return lax.rem(sub - o + n_sub, n_sub)

    def from_patch(o):
        return lax.rem(patch - o + n_patch, n_patch)

    def from_lvl(o):
        return lax.rem(lvl - o + n_lvl, n_lvl)

    def remote(src, dst, send, recv, device):
        return pltpu.make_async_remote_copy(
            src_ref=src, dst_ref=dst, send_sem=send, recv_sem=recv,
            device_id=device, device_id_type=MESH,
        )

    plan = [
        (us_hbm, w_in.at[0]), (nodes_hbm, ns), (ur_hbm, w_in.at[1]), (coarse_hbm, cs),
        (uo_hbm, w_mid.at[0]), (cs_hbm, w_in.at[2]), (cr_hbm, w_in.at[3]),
        (dr_hbm, w_in.at[4]), (co_hbm, w_mid.at[1]), (ds_hbm, w_in.at[5]),
        (do_hbm, wo_full.at[0, sub]), (bs_hbm, w_in.at[6]), (br_hbm, w_in.at[7]),
        (bo_hbm, wo_full.at[1, sub]),
    ]
    loads = [
        pltpu.make_async_copy(src, dst, load_sem.at[i]) for i, (src, dst) in enumerate(plan)
    ]
    for load in loads:
        load.start()
    (l_us, l_ns, l_ur, l_cst, l_uo, l_cs, l_cr, l_dr, l_co, l_ds, l_do, l_bs, l_br, l_bo) = loads

    barrier = pltpu.get_barrier_semaphore()
    peers = [at_sub(o) for o in range(1, n_sub)]
    peers += [at_lvl(o) for o in range(1, n_lvl)]
    peers += [at_patch(o) for o in range(1, n_patch)]
    peers += [at_block(-1), at_block(1)]
    for peer in peers:
        pl.semaphore_signal(barrier, inc=1, device_id=peer, device_id_type=MESH)
    pl.semaphore_wait(barrier, len(peers))

    share = width // n_lvl

    def wo_copy(j, o, source, index):
        mine = pl.ds(pl.multiple_of(lvl * share, share), share)
        return remote(
            source.at[mine], wo_full.at[j, index, mine],
            wo_send.at[j, o - 1], wo_recv.at[j, o - 1], at_sub(o),
        )

    def wo_pass(j, o, q, owner, holder):
        part = pl.ds(pl.multiple_of(holder * share, share), share)
        return remote(
            wo_full.at[j, owner, part], wo_full.at[j, owner, part],
            fw_send.at[j, o - 1, q - 1], fw_recv.at[j, o - 1, q - 1], at_lvl(q),
        )

    wo_src = (do_hbm, bo_hbm)

    def start_wo(j):
        for o in range(1, n_sub):
            wo_copy(j, o, wo_src[j], sub).start()

    def forward_wo(j):
        for o in range(1, n_sub):
            wo_copy(j, o, wo_src[j], from_sub(o)).wait_recv()
            for q in range(1, n_lvl):
                wo_pass(j, o, q, from_sub(o), lvl).start()

    def finish_wo(j):
        for o in range(1, n_sub):
            wo_copy(j, o, wo_src[j], sub).wait_send()
            for q in range(1, n_lvl):
                wo_pass(j, o, q, from_sub(o), lvl).wait_send()
                wo_pass(j, o, q, from_sub(o), from_lvl(q)).wait_recv()

    def split_wo(j):
        for s in range(n_sub):
            high, low = split(wo_full[j, s])
            wo_pair[j, s, 0] = high
            wo_pair[j, s, 1] = low

    start_wo(0)

    def part_copy(j, o, index):
        return remote(
            parts.at[j, index], parts.at[j, index],
            part_send.at[j, o - 1], part_recv.at[j, o - 1], at_sub(o),
        )

    def send_part(j, value):
        parts[j, sub] = value
        for o in range(1, n_sub):
            part_copy(j, o, sub).start()

    def total_part(j):
        for o in range(1, n_sub):
            part_copy(j, o, sub).wait_send()
            part_copy(j, o, from_sub(o)).wait_recv()
        total = parts[j, 0]
        for s in range(1, n_sub):
            total = total + parts[j, s]
        return total

    l_us.wait()
    l_ns.wait()
    high, low = split(ns[...])
    ns_pair[0] = high
    ns_pair[1] = low
    sender = joined(split(dot3((high, low), split(w_in[0]))))
    l_ur.wait()
    l_cst.wait()
    receiver = dot3(split(cs[...]), split(w_in[1])) + ub[...]
    hid = jnp.zeros_like(receiver)
    for k in range(children.shape[1]):
        hid = hid + silu(pick(children[:, k : k + 1], sender, 0) + receiver)
    l_uo.wait()
    send_part(0, dot3(split(hid), split(w_mid[0])))

    l_dr.wait()
    rd[...] = dot3((ns_pair[0], ns_pair[1]), split(w_in[4])) + db[...]
    l_cs.wait()
    l_cr.wait()
    w_send = split(w_in[2])
    coarse_up = cs[...] + ug[...] * layer_norm(total_part(0))

    up_pair = split(coarse_up)
    table[block] = dot3(up_pair, w_send)

    def tab_copy(o, index):
        return remote(
            table.at[index], table.at[index], tab_send.at[o - 1], tab_recv.at[o - 1], at_patch(o)
        )

    def rel_copy(o, q, index):
        return remote(
            table.at[index], table.at[index],
            rel_send.at[o, q - 1], rel_recv.at[o, q - 1], at_lvl(q),
        )

    order = sorted(range(1, n_patch), key=lambda o: min(o, n_patch - o))
    for o in order:
        tab_copy(o, block).start()
    for q in range(1, n_lvl):
        rel_copy(0, q, block).start()
    receiver = dot3(up_pair, split(w_in[3])) + cb[...]
    l_bs.wait()
    l_br.wait()
    for i in range(2):
        high, low = split(w_in[6 + i])
        bw_pair[i, 0] = high
        bw_pair[i, 1] = low
    for o in order:
        tab_copy(o, from_patch(o) * n_lvl + lvl).wait_recv()
        for q in range(1, n_lvl):
            rel_copy(o, q, from_patch(o) * n_lvl + lvl).start()
    for q in range(1, n_lvl):
        rel_copy(0, q, patch * n_lvl + from_lvl(q)).wait_recv()
    for o in order:
        for q in range(1, n_lvl):
            rel_copy(o, q, from_patch(o) * n_lvl + from_lvl(q)).wait_recv()

    cells = table.shape[1]
    chunk = max(d for d in range(1, blocks + 1) if blocks % d == 0 and d * cells <= 512)
    picked = [None] * coarse_links.shape[1]
    for c in range(0, blocks, chunk):
        rows_pair = joined(split(table[c : c + chunk].reshape(chunk * cells, width)))
        for k in range(coarse_links.shape[1]):
            got = pick(coarse_links[:, k : k + 1], rows_pair, c * cells)
            picked[k] = got if picked[k] is None else picked[k] + got
    hid = jnp.zeros_like(receiver)
    for got in picked:
        hid = hid + silu(got + receiver)
    l_co.wait()
    send_part(1, dot3(split(hid), split(w_mid[1])))
    start_wo(1)
    for o in order:
        tab_copy(o, block).wait_send()
        for q in range(1, n_lvl):
            rel_copy(o, q, from_patch(o) * n_lvl + lvl).wait_send()
    for q in range(1, n_lvl):
        rel_copy(0, q, block).wait_send()

    l_do.wait()
    forward_wo(0)
    l_ds.wait()
    w_send = split(w_in[5])
    new_coarse = coarse_up + cg[...] * layer_norm(total_part(1))
    out_coarse[...] = new_coarse

    def hid_copy(j, t, o, index):
        part = pl.ds(t * tile, tile)
        return remote(
            hidden.at[j, index, part], hidden.at[j, index, part],
            hid_send.at[j, t, o - 1], hid_recv.at[j, t, o - 1], at_sub(o),
        )

    def send_hidden(j, t, value):
        hidden[j, sub, t * tile : (t + 1) * tile] = value
        for o in range(1, n_sub):
            hid_copy(j, t, o, sub).start()

    def update(j, t):
        for o in range(1, n_sub):
            hid_copy(j, t, o, from_sub(o)).wait_recv()
        total = None
        for s in range(n_sub):
            term = dot3(
                split(hidden[j, s, t * tile : (t + 1) * tile]), (wo_pair[j, s, 0], wo_pair[j, s, 1])
            )
            total = term if total is None else total + term
        return layer_norm(total)

    def interact(j, t, links, rows_pair, base, receiver):
        hid = jnp.zeros_like(receiver)
        for k in range(links.shape[1]):
            column = links[t * tile : (t + 1) * tile, k : k + 1]
            hid = hid + silu(pick(column, rows_pair, base) + receiver)
        send_hidden(j, t, hid)

    rows_pair = joined(split(dot3(split(new_coarse), w_send)))
    ends = [0, tiles - 1] + list(range(1, tiles - 1))
    for t in ends:
        interact(0, t, down_sources, rows_pair, 0, rd[t * tile : (t + 1) * tile])
    finish_wo(0)
    split_wo(0)

    def halo_copy(side):
        return remote(
            halo_out.at[side], halo_in.at[1 - side],
            halo_send.at[side], halo_recv.at[side], at_block(2 * side - 1),
        )

    for t in ends:
        part = slice(t * tile, (t + 1) * tile)
        value = ns[part] + dg[...] * update(0, t)
        nd[part] = value
        pair = split(value)
        sent = dot3(pair, (bw_pair[0, 0], bw_pair[0, 1]))
        if t == 0:
            halo_out[0] = sent[:rim]
            halo_copy(0).start()
        if t == tiles - 1:
            halo_out[1] = sent[tile - rim :]
            halo_copy(1).start()
        ext[rim + t * tile : rim + (t + 1) * tile] = joined(split(sent))
        rb[part] = dot3(pair, (bw_pair[1, 0], bw_pair[1, 1])) + bb[...]

    inner = list(range(1, tiles - 1)) + [0, tiles - 1]
    for t in inner:
        if t == 0:
            halo_copy(1).wait_recv()
            ext[:rim] = joined(split(halo_in[0]))
        if t == tiles - 1:
            halo_copy(0).wait_recv()
            ext[rim + rows :] = joined(split(halo_in[1]))
        if t == inner[1]:
            l_bo.wait()
            forward_wo(1)
        interact(
            1, t, bottom_links, ext[t * tile : (t + 1) * tile + 2 * rim], t * tile,
            rb[t * tile : (t + 1) * tile],
        )
    finish_wo(1)
    split_wo(1)
    for t in inner:
        part = slice(t * tile, (t + 1) * tile)
        out_nodes[part] = nd[part] + bg[...] * update(1, t)
    halo_copy(0).wait_send()
    halo_copy(1).wait_send()
    for j in range(2):
        for t in range(tiles):
            for o in range(1, n_sub):
                hid_copy(j, t, o, sub).wait_send()


def body(
    node_states, coarse_states, children, down_sources, bottom_links, coarse_links,
    upward_sender, upward_receiver, upward_bias, upward_output, upward_gain,
    coarse_sender, coarse_receiver, coarse_bias, coarse_output, coarse_gain,
    downward_sender, downward_receiver, downward_bias, downward_output, downward_gain,
    bottom_sender, bottom_receiver, bottom_bias, bottom_output, bottom_gain,
):
    n_patch, n_sub, n_lvl = (lax.axis_size(a) for a in ("patch", "sub", "lvl"))
    rows, lat = node_states.shape
    cells = coarse_states.shape[0]
    width = upward_sender.shape[1]
    rim = rows // 4
    tile = rim
    tiles = rows // tile
    blocks = n_patch * n_lvl
    others = n_sub - 1
    row = lambda v: v.reshape(1, -1)
    dma = pltpu.SemaphoreType.DMA
    vmem = pl.BlockSpec(memory_space=pltpu.VMEM)
    anywhere = pl.BlockSpec(memory_space=pl.ANY)
    return pl.pallas_call(
        functools.partial(kernel, n_patch, n_sub, n_lvl, rim, tile),
        out_shape=(
            jax.ShapeDtypeStruct((rows, lat), f32),
            jax.ShapeDtypeStruct((cells, lat), f32),
        ),
        in_specs=[anywhere] * 14 + [vmem] * 12,
        out_specs=(vmem, vmem),
        scratch_shapes=[
            pltpu.VMEM((rows, lat), f32),
            pltpu.VMEM((cells, lat), f32),
            pltpu.VMEM((8, lat, width), f32),
            pltpu.VMEM((2, width, lat), f32),
            pltpu.VMEM((2, n_sub, width, lat), f32),
            pltpu.VMEM((2, n_sub, 2, width, lat), bf16),
            pltpu.VMEM((2, 2, lat, width), bf16),
            pltpu.VMEM((2, rows, lat), bf16),
            pltpu.VMEM((rows, width), f32),
            pltpu.VMEM((rows, width), f32),
            pltpu.VMEM((rows, lat), f32),
            pltpu.VMEM((rows + 2 * rim, 2 * width), bf16),
            pltpu.VMEM((2, rim, width), f32),
            pltpu.VMEM((2, rim, width), f32),
            pltpu.VMEM((blocks, cells, width), f32),
            pltpu.VMEM((2, n_sub, cells, lat), f32),
            pltpu.VMEM((2, n_sub, rows, width), f32),
            dma((14,)),
            dma((2, others)),
            dma((2, others)),
            dma((2, others, n_lvl - 1)),
            dma((2, others, n_lvl - 1)),
            dma((2, others)),
            dma((2, others)),
            dma((n_patch - 1,)),
            dma((n_patch - 1,)),
            dma((n_patch, n_lvl - 1)),
            dma((n_patch, n_lvl - 1)),
            dma((2, tiles, others)),
            dma((2, tiles, others)),
            dma((2,)),
            dma((2,)),
        ],
        compiler_params=pltpu.CompilerParams(
            collective_id=0, has_side_effects=True, vmem_limit_bytes=60 * 1024 * 1024
        ),
        name="sweep",
    )(
        node_states, coarse_states,
        upward_sender, upward_receiver, upward_output,
        coarse_sender, coarse_receiver, coarse_output,
        downward_sender, downward_receiver, downward_output,
        bottom_sender, bottom_receiver, bottom_output,
        children, down_sources, bottom_links, coarse_links,
        row(upward_bias), row(upward_gain), row(coarse_bias), row(coarse_gain),
        row(downward_bias), row(downward_gain), row(bottom_bias), row(bottom_gain),
    )


def solution(mesh):
    rows = P(("parts", "patch", "lvl"), None)
    links = P(("patch", "lvl"), None)
    weights = (P(None, "sub"), P(None, "sub"), P("sub"), P("sub", None), P())
    in_specs = (rows, rows, links, links, links, links) + weights * 4
    return jax.shard_map(
        body, mesh=mesh, in_specs=in_specs, out_specs=(rows, rows), check_vma=False
    )
```

time: 236 us -> 72.3 us (0.31)
  waiting for transfers between devices: 125 us -> 0 us
  Pallas kernels: 0 us -> 64.6 us
  other arithmetic: 29.8 us -> 0 us
  local copies, waits for them, and re-layouts: 30.7 us -> 6.76 us
  matrix products: 17.2 us -> 0 us
  blocking collectives: 14.7 us -> 0 us
  between operations: 14.4 us -> 0.66 us
  starting transfers between devices: 3.93 us -> 0 us
    psum x4 -> x0, waiting for transfers between devices: 123 us -> none  [finish(): summed = lax.psum(partial_value, 'sub')]
    pallas_call x0 -> x1, Pallas kernels: none -> 64.6 us  [body(): pl.pallas_call(functools.partial(kernel, n_patch, n_sub, n_lvl, rim, tile...]
    gather x8 -> x0, local copies, waits for them, and re-layouts: 28.7 us -> none  [the longest x2 16.9 us: body(): picked = jnp.take(sender_rows, bottom_links, axis=0)]
    reduce_sum x12 -> x0, other arithmetic: 22.3 us -> none  [the longest x4 12.4 us: hidden_total(): return jnp.sum(jax.nn.silu(picked + receiver_rows[:, None, :]), axis=1)]
    dot_general x12 -> x0, matrix products: 17.2 us -> none  [project(): jnp.dot(states, weights, precision=highest, preferred_element_type=jnp.fl...]
    all_gather x1 -> x0, blocking collectives: 14.7 us -> none  [body(): lax.all_gather(own_projection, ('patch', 'lvl'), axis=0, tiled=True)]
    unnamed x42 -> x16, local copies, waits for them, and re-layouts: 0.13 us -> 6.76 us
    add x4 -> x0, other arithmetic: 5.93 us -> none  [finish(): return receivers + gain_vector * layer_norm(summed)]
  transfers between devices with their start and end apart: 6 -> 0, of which waited for: 5 -> 0; matrix products, arithmetic and copies ran while one was open for 2% -> 0% of each run, Pallas kernels for 0% -> 0%
where the time goes in v1:
time: 72.3 us; the launch traced here: 72.1 us
  Pallas kernels  64.6 us (89%)
  local copies, waits for them, and re-layouts  6.76 us (9%)
    pallas_call x1, Pallas kernels, body(): pl.pallas_call(functools.partial(kernel, n_patch, n_sub, n_lvl, rim, tile...  64.6 us
    unnamed x16, local copies, waits for them, and re-layouts  6.76 us

profile of v1, /device:TPU:0, one launch (start us, length us, event | category | flops | bytes accessed | tf_op | source)
XLA Modules:
  0.0 72.1 jit_solution(543243742675530511)
XLA Ops:
  0.6 0.0 copy-start.3
  0.6 0.7 copy-done.3
  1.3 0.0 copy-start.4
  1.3 0.7 copy.28.children
  2.0 0.0 copy-done.4
  2.0 0.0 copy-start.2
  2.0 0.7 copy.31.coarse_links
  2.7 0.0 copy-done.2
  2.7 0.0 copy-start.1
  2.7 0.9 %copy.29.down_sources = s32[512,3]{1,0:T(8,128)} copy(s32[512,3]{0,1:T(4,128)S(1)} %copy-done.2) | data formatting | bytes 12288 | tf_op args[3]
  3.6 0.0 copy-done.1
  3.6 0.8 %copy.30.bottom_links = s32[512,6]{1,0:T(8,128)} copy(s32[512,6]{0,1:T(8,128)S(1)} %copy-done.1) | data formatting | bytes 24576 | tf_op args[4]
  4.4 64.6 %sweep.1 = (f32[512,512]{1,0:T(8,128)}, f32[64,512]{1,0:T(8,128)}) custom-call(f32[512,512]{1,0:T(8,128)} %nodes_hbm.1, f32[64,512]{1,0:T(8,128)} %coarse_hbm.1, f32[512,256]{1,0:T(8,128)} %us_hbm.1, f32[512,256]{1,0:T(8,128)} %ur_hbm.1, f32[256,512]{1,0:T(8,128)} %uo_hbm.1, f32[512,256]{1,0:T(8,128)} %cs_hbm.1, f32[512,256]{1,0:T(8,128)} %cr_hbm.1, ...), custom_call_target="tpu_custom_call" | custom-call | tf_op jit(solution)/shard_map/sweep/pallas_call | solution.py:390
  69.1 0.0 copy-start
  69.1 2.3 %copy.34 = f32[512,512]{1,0:T(8,128)} copy(f32[512,512]{1,0:T(8,128)} %get-tuple-element.4) | data formatting | bytes 2097152
  71.4 0.0 copy-done
  71.4 0.7 copy.35
Async XLA Ops:
  0.6 0.7 copy-start.3
  1.3 0.7 copy-start.4
  2.0 0.7 copy-start.2
  2.7 0.9 %copy-start.1 = (s32[512,6]{0,1:T(8,128)S(1)}, s32[512,6]{0,1:T(8,128)}, u32[]{:S(2)}) copy-start(s32[512,6]{0,1:T(8,128)} %param.30) | copy-start | bytes 36868
  69.1 2.3 %copy-start = (f32[64,512]{1,0:T(8,128)S(1)}, f32[64,512]{1,0:T(8,128)}, u32[]{:S(2)}) copy-start(f32[64,512]{1,0:T(8,128)} %get-tuple-element.5) | copy-start | bytes 393220

commit v2 on v1

--- a/solution.py
+++ b/solution.py
@@ -72,6 +72,9 @@
     part_send, part_recv, tab_send, tab_recv, rel_send, rel_recv,
     hid_send, hid_recv, halo_send, halo_recv,
 ):
+    children, down_sources, bottom_links, coarse_links = (
+        jnp.transpose(links[...]) for links in (children, down_sources, bottom_links, coarse_links)
+    )
     patch = lax.axis_index("patch")
     sub = lax.axis_index("sub")
     lvl = lax.axis_index("lvl")
@@ -119,7 +122,8 @@
     loads = [
         pltpu.make_async_copy(src, dst, load_sem.at[i]) for i, (src, dst) in enumerate(plan)
     ]
-    for load in loads:
+    early = 5
+    for load in loads[:early]:
         load.start()
     (l_us, l_ns, l_ur, l_cst, l_uo, l_cs, l_cr, l_dr, l_co, l_ds, l_do, l_bs, l_br, l_bo) = loads
 
@@ -173,8 +177,6 @@
             wo_pair[j, s, 0] = high
             wo_pair[j, s, 1] = low
 
-    start_wo(0)
-
     def part_copy(j, o, index):
         return remote(
             parts.at[j, index], parts.at[j, index],
@@ -197,6 +199,8 @@
 
     l_us.wait()
     l_ns.wait()
+    for load in loads[early:]:
+        load.start()
     high, low = split(ns[...])
     ns_pair[0] = high
     ns_pair[1] = low
@@ -236,6 +240,8 @@
         tab_copy(o, block).start()
     for q in range(1, n_lvl):
         rel_copy(0, q, block).start()
+    start_wo(0)
+    start_wo(1)
     receiver = dot3(up_pair, split(w_in[3])) + cb[...]
     l_bs.wait()
     l_br.wait()
@@ -266,7 +272,6 @@
         hid = hid + silu(got + receiver)
     l_co.wait()
     send_part(1, dot3(split(hid), split(w_mid[1])))
-    start_wo(1)
     for o in order:
         tab_copy(o, block).wait_send()
         for q in range(1, n_lvl):
@@ -275,7 +280,9 @@
         rel_copy(0, q, block).wait_send()
 
     l_do.wait()
+    l_bo.wait()
     forward_wo(0)
+    forward_wo(1)
     l_ds.wait()
     w_send = split(w_in[5])
     new_coarse = coarse_up + cg[...] * layer_norm(total_part(1))
@@ -311,20 +318,13 @@
             hid = hid + silu(pick(column, rows_pair, base) + receiver)
         send_hidden(j, t, hid)
 
-    rows_pair = joined(split(dot3(split(new_coarse), w_send)))
-    ends = [0, tiles - 1] + list(range(1, tiles - 1))
-    for t in ends:
-        interact(0, t, down_sources, rows_pair, 0, rd[t * tile : (t + 1) * tile])
-    finish_wo(0)
-    split_wo(0)
-
     def halo_copy(side):
         return remote(
             halo_out.at[side], halo_in.at[1 - side],
             halo_send.at[side], halo_recv.at[side], at_block(2 * side - 1),
         )
 
-    for t in ends:
+    def descend(t):
         part = slice(t * tile, (t + 1) * tile)
         value = ns[part] + dg[...] * update(0, t)
         nd[part] = value
@@ -339,24 +339,32 @@
         ext[rim + t * tile : rim + (t + 1) * tile] = joined(split(sent))
         rb[part] = dot3(pair, (bw_pair[1, 0], bw_pair[1, 1])) + bb[...]
 
-    inner = list(range(1, tiles - 1)) + [0, tiles - 1]
-    for t in inner:
+    def bottom(t):
         if t == 0:
             halo_copy(1).wait_recv()
             ext[:rim] = joined(split(halo_in[0]))
         if t == tiles - 1:
             halo_copy(0).wait_recv()
             ext[rim + rows :] = joined(split(halo_in[1]))
-        if t == inner[1]:
-            l_bo.wait()
-            forward_wo(1)
         interact(
             1, t, bottom_links, ext[t * tile : (t + 1) * tile + 2 * rim], t * tile,
             rb[t * tile : (t + 1) * tile],
         )
-    finish_wo(1)
-    split_wo(1)
-    for t in inner:
+
+    rows_pair = joined(split(dot3(split(new_coarse), w_send)))
+    for t in range(tiles):
+        interact(0, t, down_sources, rows_pair, 0, rd[t * tile : (t + 1) * tile])
+    for j in range(2):
+        finish_wo(j)
+        split_wo(j)
+    for t in range(tiles):
+        descend(t)
+        if 2 <= t < tiles - 1:
+            bottom(t - 1)
+    last = list(range(max(tiles - 2, 1), tiles)) + [0]
+    for t in last:
+        bottom(t)
+    for t in list(range(1, tiles)) + [0]:
         part = slice(t * tile, (t + 1) * tile)
         out_nodes[part] = nd[part] + bg[...] * update(1, t)
     halo_copy(0).wait_send()
@@ -439,7 +447,7 @@
         coarse_sender, coarse_receiver, coarse_output,
         downward_sender, downward_receiver, downward_output,
         bottom_sender, bottom_receiver, bottom_output,
-        children, down_sources, bottom_links, coarse_links,
+        children.T, down_sources.T, bottom_links.T, coarse_links.T,
         row(upward_bias), row(upward_gain), row(coarse_bias), row(coarse_gain),
         row(downward_bias), row(downward_gain), row(bottom_bias), row(bottom_gain),
     )

time: 72.3 us -> 59.5 us (0.82)
  Pallas kernels: 64.6 us -> 55.7 us
  local copies, waits for them, and re-layouts: 6.76 us -> 2.96 us
    pallas_call x1, Pallas kernels: 64.6 us -> 55.7 us  [body(): pl.pallas_call(functools.partial(kernel, n_patch, n_sub, n_lvl, rim, tile...]
    unnamed x16 -> x4, local copies, waits for them, and re-layouts: 6.76 us -> 2.96 us
where the time goes in v2:
time: 59.5 us; the launch traced here: 59.3 us
  Pallas kernels  55.7 us (94%)
  local copies, waits for them, and re-layouts  2.96 us (5%)
  between operations  0.66 us (1%)
    pallas_call x1, Pallas kernels, body(): pl.pallas_call(functools.partial(kernel, n_patch, n_sub, n_lvl, rim, tile...  55.7 us
    unnamed x4, local copies, waits for them, and re-layouts  2.96 us

profile of v2, /device:TPU:0, one launch (start us, length us, event | category | flops | bytes accessed | tf_op | source)
XLA Modules:
  0.0 59.3 jit_solution(1183640323604550393)
XLA Ops:
  0.6 55.7 %sweep.1 = (f32[512,512]{1,0:T(8,128)}, f32[64,512]{1,0:T(8,128)}) custom-call(f32[512,512]{1,0:T(8,128)} %nodes_hbm.1, f32[64,512]{1,0:T(8,128)} %coarse_hbm.1, f32[512,256]{1,0:T(8,128)} %us_hbm.1, f32[512,256]{1,0:T(8,128)} %ur_hbm.1, f32[256,512]{1,0:T(8,128)} %uo_hbm.1, f32[512,256]{1,0:T(8,128)} %cs_hbm.1, f32[512,256]{1,0:T(8,128)} %cr_hbm.1, ...), custom_call_target="tpu_custom_call" | custom-call | tf_op jit(solution)/shard_map/sweep/pallas_call | solution.py:398
  56.3 0.0 copy-start
  56.3 2.3 %copy.30 = f32[512,512]{1,0:T(8,128)} copy(f32[512,512]{1,0:T(8,128)} %get-tuple-element.4) | data formatting | bytes 2097152
  58.6 0.0 copy-done
  58.6 0.7 %copy.31 = f32[64,512]{1,0:T(8,128)} copy(f32[64,512]{1,0:T(8,128)S(1)} %copy-done) | data formatting | bytes 262144
Async XLA Ops:
  56.3 2.3 %copy-start = (f32[64,512]{1,0:T(8,128)S(1)}, f32[64,512]{1,0:T(8,128)}, u32[]{:S(2)}) copy-start(f32[64,512]{1,0:T(8,128)} %get-tuple-element.5) | copy-start | bytes 393220
